TPU v7x, 256 devices: a whole 4x4x8 slice. The times are simulated.
256 devices in a mesh: group: 8 (over x, core), member: 32 (over y, z).
Axes of the slice: x: 4, y: 4, z: 8, core: 2. Of those that a mesh axis runs over, the one named last changes fastest.
Arguments:
- q_rows: bfloat16 [65536, 8192], P(('group', 'member')), may hold values from -36 to 36
- own_kv: bfloat16 [65536, 1024], P(('group', 'member')), may hold values from -6 to 6
- cache: bfloat16 [1024, 64, 1024], P(('group', 'member')), may hold values from -6 to 6
- recomp_hidden: bfloat16 [512, 8, 16, 4096], P(('group', 'member')), may hold values from -6 to 6
- w_kv: bfloat16 [4096, 1024], P('member', 'group'), may hold values from -0.09375 to 0.09375
- retrieval: int32 [512, 8], P(('group', 'member')), may hold values from 0 to 127, as said below
- positions: int32 [512, 8, 16], P(('group', 'member')), may hold values from 0 to 63, as said below
Outputs:
- attn_out: bfloat16 [65536, 8192], P(('group', 'member'))
Inputs may be any that keep to these rules, and one draw needn't show every extreme that they name: `retrieval`: the 8 passages of one query are different. Passage i of a group's corpus is held by the device of member index i // 4 in that group. The queries of one device name at most 1 passages held by any one device, and this bound is reached. The 16 positions of one retrieved passage are different.
All inputs are finite; a program needn't handle non-finite values.
Results may differ from a plain program's by a relative error of at most 0.0054.
Values may be sent and summed in bfloat16 or wider, within the bound.
A program may use at most 128 MiB of HBM per device.

v0:
```python
import jax
import jax.numpy as jnp
from jax import lax
from jax.sharding import PartitionSpec as P

D = 4096
HQ = 64
KVH = 4
HD = 128
TOPP = 8
QLEN = 128
PLEN = 64
RECOMP = 16
EPSILON = 1e-06


def local(q_rows, own_kv, cache, recomp_hidden, w_kv, retrieval, positions):
    query_count = retrieval.shape[0]
    requests = query_count * TOPP
    kv_width = 2 * KVH * HD
    grouped = HQ // KVH
    span_keys = TOPP * PLEN + QLEN
    scale = 1.0 / HD**0.5
    row_count = requests * RECOMP
    hidden = recomp_hidden.reshape(row_count, D).astype(jnp.float32)
    normed = (
        hidden * lax.rsqrt(jnp.mean(hidden * hidden, axis=1, keepdims=True) + EPSILON)
    ).astype(jnp.bfloat16)
    head_columns = lax.all_gather(w_kv, "group", axis=1, tiled=True)
    projected = jnp.dot(
        normed,
        lax.all_gather(head_columns, "member", axis=0, tiled=True),
        preferred_element_type=jnp.float32,
    )
    recomputed = projected.astype(jnp.bfloat16).reshape(requests, RECOMP, kv_width)
    wanted = retrieval.reshape(requests)
    pass_local = cache.shape[0]
    holders_count = lax.axis_size("member")
    my_index = lax.axis_index("member")
    capacity = -(-requests // holders_count)
    request_table = lax.all_gather(wanted.reshape(1, requests), "member", axis=0, tiled=True)
    mine_mask = request_table // pass_local == my_index
    earlier_mask = (jnp.arange(requests)[:, None] < jnp.arange(requests)[None, :]).astype(jnp.int32)
    slot_rank = jnp.dot(mine_mask.astype(jnp.int32), earlier_mask)
    slot_table = mine_mask[:, None, :] & (
        slot_rank[:, None, :] == jnp.arange(capacity)[None, :, None]
    )
    local_index = jnp.sum(
        jnp.where(slot_table, (request_table % pass_local)[:, None, :], 0), axis=2
    )
    slot_filled = jnp.any(slot_table, axis=2)
    outgoing = jnp.where(
        slot_filled[:, :, None, None], cache[local_index], jnp.zeros((), cache.dtype)
    )
    arrived = lax.all_to_all(outgoing, "member", split_axis=0, concat_axis=0, tiled=True)
    holder_of = wanted // pass_local
    same_holder = holder_of[:, None] == holder_of[None, :]
    before_me = jnp.arange(requests)[None, :] < jnp.arange(requests)[:, None]
    copy_rank = jnp.sum((same_holder & before_me).astype(jnp.int32), axis=1)
    blocks = arrived.reshape(holders_count * capacity, PLEN, kv_width)[
        holder_of * capacity + copy_rank
    ]
    spots = positions.reshape(requests, RECOMP)
    onehot = spots[:, :, None] == jnp.arange(PLEN)[None, None, :]
    covered = jnp.any(onehot, axis=1)
    placed = jnp.einsum(
        "krp,kre->kpe", onehot.astype(jnp.bfloat16), recomputed, preferred_element_type=jnp.float32
    ).astype(jnp.bfloat16)
    context = jnp.where(covered[:, :, None], placed, blocks).reshape(
        query_count, TOPP * PLEN, kv_width
    )
    context = jnp.concatenate([context, own_kv.reshape(query_count, QLEN, kv_width)], axis=1)
    keys = context[:, :, : KVH * HD].reshape(query_count, span_keys, KVH, HD)
    values = context[:, :, KVH * HD :].reshape(query_count, span_keys, KVH, HD)
    queries = q_rows.reshape(query_count, QLEN, KVH, grouped, HD)
    token_pos = jnp.arange(QLEN)[:, None]
    key_pos = jnp.arange(span_keys)[None, :]
    visible = (key_pos < TOPP * PLEN) | (key_pos - TOPP * PLEN <= token_pos)

    def attend(operands):
        query_block, key_block, value_block = operands
        scores = (
            jnp.einsum("tkgd,skd->kgts", query_block, key_block, preferred_element_type=jnp.float32)
            * scale
        )
        scores = jnp.where(visible, scores, -jnp.inf)
        peak = jnp.max(scores, axis=-1, keepdims=True)
        expd = jnp.exp(scores - peak)
        probs = (expd / jnp.sum(expd, axis=-1, keepdims=True)).astype(jnp.bfloat16)
        output = jnp.einsum(
            "kgts,skd->tkgd", probs, value_block, preferred_element_type=jnp.float32
        )
        return output.astype(jnp.bfloat16).reshape(QLEN, HQ * HD)

    results = lax.map(attend, (queries, keys, values))
    return results.reshape(query_count * QLEN, HQ * HD)


def solution(mesh):
    placed = (
        P(("group", "member"), None),
        P(("group", "member"), None),
        P(("group", "member"), None, None),
        P(("group", "member"), None, None, None),
        P("member", "group"),
        P(("group", "member"), None),
        P(("group", "member"), None, None),
    )
    return jax.shard_map(
        local, mesh=mesh, in_specs=placed, out_specs=P(("group", "member"), None), check_vma=False
    )
```

profile of v0, /device:TPU:32, one launch (start us, length us, event | category | flops | bytes accessed | tf_op | source)
XLA Modules:
  0.0 287.2 jit_solution(2852515802772880683)
XLA Ops:
  6.5 13.6 %all_gather.9 = bf16[128,1024]{1,0:T(8,128)(2,1)} all-gather(bf16[128,128]{1,0:T(8,128)(2,1)} %param.13), channel_id=1, replica_groups=mesh['group'=8,'member'=32] {'group'}, dimensions={1}, use_global_device_ids=true | all-gather | bytes 294912 | tf_op jit(solution)/shard_map/all_gather | solution.py:29
  21.0 40.2 %all-gather = s32[32,1,16]{2,1,0:T(1,128)S(1)} all-gather(s32[1,1,16]{2,1,0:T(1,128)S(1)} %reshape.252), channel_id=1, replica_groups=mesh['group'=8,'member'=32] {'member'}, dimensions={0}, use_global_device_ids=true | all-gather | bytes 2112 | tf_op jit(solution)/shard_map/all_gather | solution.py:41
  61.5 2.8 gather_fusion
  64.4 4.5 %bitcast_select_fusion.4 = bf16[32,1,64,1024]{3,2,1,0:T(8,128)(2,1)} fusion(bf16[32,64,1024]{2,1,0:T(8,128)(2,1)} %gather_fusion, pred[32]{0:T(512)(128)(4,1)S(1)} %reduce_or.19), kind=kLoop, calls=%fused_computation.31 | loop fusion | flops 2097152 | bytes 8388640 | tf_op jit(solution)/shard_map/jit(_where)/select_n | solution.py:52
  68.9 8.1 %all-to-all-start = ((bf16[32,1,64,1024]{3,2,1,0:T(8,128)(2,1)}), bf16[32,1,64,1024]{3,2,1,0:T(8,128)(2,1)}, u32[]{:S(2)}, u32[]{:S(2)}) async-start(bf16[32,1,64,1024]{3,2,1,0:T(8,128)(2,1)} %bitcast_select_fusion.4), calls=%async_computation | async-start | bytes 8388608 | tf_op jit(solution)/shard_map/all_to_all | solution.py:55
  78.1 5.4 %copy.46 = bf16[32,8,64,128]{3,2,1,0:T(8,128)(2,1)} copy(bf16[32,8,64,128]{3,1,2,0:T(8,128)(2,1)} %bitcast.134) | data formatting | bytes 8388608
  83.8 1.9 fusion.30
  85.7 118.0 %all-to-all-done = bf16[32,1,64,1024]{3,2,1,0:T(8,128)(2,1)} async-done(((bf16[32,1,64,1024]{3,2,1,0:T(8,128)(2,1)}), bf16[32,1,64,1024]{3,2,1,0:T(8,128)(2,1)}, u32[]{:S(2)}, u32[]{:S(2)}) %all-to-all-start) | async-done | bytes 4194336 | tf_op jit(solution)/shard_map/all_to_all | solution.py:55
  203.7 2.9 gather_fusion.1
  206.6 6.3 %convolution_convert_fusion = bf16[256,1024]{1,0:T(8,128)(2,1)S(1)} fusion(bf16[256,4096]{1,0:T(8,128)(2,1)} %fusion.30, bf16[4096,1024]{1,0:T(8,128)(2,1)} %all-gather.3.cloned.1.call-done), kind=kOutput, calls=%fused_computation.40 | convolution fusion | flops 2147745792 | bytes 11010048 | tf_op jit(solution)/shard_map/dot_general | solution.py:30
  213.0 2.6 convert_select_fusion
  215.6 2.9 copy.34
  218.4 1.7 pad_maximum_fusion
  220.2 59.2 %while.11 = (s32[]{:T(128)}, bf16[2,128,8192]{2,1,0:T(8,128)(2,1)}, bf16[2,640,4,128]{1,3,2,0:T(8,128)(2,1)}, bf16[2,640,4,128]{1,3,2,0:T(8,128)(2,1)}, bf16[2,1...) while((s32[]{:T(128)}, bf16[2,128,8192]{2,1,0:T(8,128)(2,1)}, ...), condition=%wide.region_8.9_spmd.clone, body=%wide.region_5.8_spmd.clone.sunk | while | flops 2717024768 | bytes 60265176 | solution.py:95
  220.2 2.0 constant_dynamic-slice_fusion.2
  222.4 12.5 %fusion.73 = (f32[4,16,128]{2,1,0:T(8,128)S(1)}, f32[4,16,128,640]{2,3,1,0:T(8,128)}) fusion(pred[128,640]{0,1:T(8,128)(4,1)S(1)} %fusion.72, bf16[1,128,4,16,128]{4,3,2,1,0:T(8,128)(2,1)S(1)} %constant_dynamic-slice_fusion.2, bf16[2,640,4,128]{1,3,2,0:T(8,128)(2,1)} %get-tuple-element.170, s32[]{:T(128)} %get-tuple-element.159), kind=kOutput, calls=%fused_computation.92.clone.1 | convolution fusion | flops 1363149440 | bytes 23839232 | tf_op jit(solution)/shard_map/while/body/eval_jaxpr/sub | solution.py:88
  234.9 10.4 %fusion.74 = bf16[4,128,16,128]{3,1,2,0:T(8,128)(2,1)} fusion(f32[4,16,128,640]{2,3,1,0:T(8,128)} %get-tuple-element.149, f32[4,16,128]{2,1,0:T(8,128)S(1)} %get-tuple-element.150, bf16[2,640,4,128]{1,3,2,0:T(8,128)(2,1)} %get-tuple-element.169, s32[]{:T(128)} %get-tuple-element.159), kind=kOutput, calls=%fused_computation.14.clone.1 | convolution fusion | flops 1353711616 | bytes 23757312 | tf_op jit(solution)/shard_map/while/body/eval_jaxpr/kgts,skd->tkgd/dot_general | solution.py:90
  245.4 2.9 %copy.61 = bf16[1,128,8192]{2,1,0:T(8,128)(2,1)S(1)} copy(bf16[1,128,8192]{1,2,0:T(8,128)(2,1)} %bitcast.131) | data formatting | bytes 4194304 | tf_op jit(solution)/shard_map/while/body/jit(dynamic_update_index_in_dim)/dynamic_update_slice | solution.py:95
  248.3 1.5 constant_dynamic-update-slice_fusion.2
  249.8 2.0 constant_dynamic-slice_fusion.2
  252.0 12.5 %fusion.73 = (f32[4,16,128]{2,1,0:T(8,128)S(1)}, f32[4,16,128,640]{2,3,1,0:T(8,128)}) fusion(pred[128,640]{0,1:T(8,128)(4,1)S(1)} %fusion.72, bf16[1,128,4,16,128]{4,3,2,1,0:T(8,128)(2,1)S(1)} %constant_dynamic-slice_fusion.2, bf16[2,640,4,128]{1,3,2,0:T(8,128)(2,1)} %get-tuple-element.170, s32[]{:T(128)} %get-tuple-element.159), kind=kOutput, calls=%fused_computation.92.clone.1 | convolution fusion | flops 1363149440 | bytes 23839232 | tf_op jit(solution)/shard_map/while/body/eval_jaxpr/sub | solution.py:88
  264.5 10.4 %fusion.74 = bf16[4,128,16,128]{3,1,2,0:T(8,128)(2,1)} fusion(f32[4,16,128,640]{2,3,1,0:T(8,128)} %get-tuple-element.149, f32[4,16,128]{2,1,0:T(8,128)S(1)} %get-tuple-element.150, bf16[2,640,4,128]{1,3,2,0:T(8,128)(2,1)} %get-tuple-element.169, s32[]{:T(128)} %get-tuple-element.159), kind=kOutput, calls=%fused_computation.14.clone.1 | convolution fusion | flops 1353711616 | bytes 23757312 | tf_op jit(solution)/shard_map/while/body/eval_jaxpr/kgts,skd->tkgd/dot_general | solution.py:90
  275.0 2.9 %copy.61 = bf16[1,128,8192]{2,1,0:T(8,128)(2,1)S(1)} copy(bf16[1,128,8192]{1,2,0:T(8,128)(2,1)} %bitcast.131) | data formatting | bytes 4194304 | tf_op jit(solution)/shard_map/while/body/jit(dynamic_update_index_in_dim)/dynamic_update_slice | solution.py:95
  277.9 1.5 constant_dynamic-update-slice_fusion.2
  (37 shorter events, 4.0 us)
Async XLA Ops:
  6.5 55.0 %copy-start = (bf16[4,64,1024]{2,1,0:T(8,128)(2,1)S(1)}, bf16[4,64,1024]{2,1,0:T(8,128)(2,1)}, u32[]{:S(2)}) copy-start(bf16[4,64,1024]{2,1,0:T(8,128)(2,1)} %param.11) | copy-start | bytes 1572868
  6.5 200.1 %all-gather.3.cloned.1.call-start = ((), (), s32[]{:S(2)}) async-start(), calls=%async_computation.1 | async-start | bytes 8650752 | tf_op jit(solution)/shard_map/all_gather | solution.py:32
  68.9 8.1 %copy-start.5 = (s32[2,8]{1,0:T(2,128)S(1)}, s32[2,8]{1,0:T(2,128)}, u32[]{:S(2)}) copy-start(s32[2,8]{1,0:T(2,128)} %param.14) | copy-start | bytes 196
  68.9 8.3 %copy-start.2 = (bf16[2,8,16,4096]{3,2,1,0:T(8,128)(2,1)S(1)}, bf16[2,8,16,4096]{3,2,1,0:T(8,128)(2,1)}, u32[]{:S(2)}) copy-start(bf16[2,8,16,4096]{3,2,1,0:T(8,128)(2,1)} %param.12) | copy-start | bytes 6291460
  68.9 8.9 %copy-start.3 = (bf16[256,1024]{1,0:T(8,128)(2,1)S(1)}, bf16[256,1024]{1,0:T(8,128)(2,1)}, u32[]{:S(2)}) copy-start(bf16[256,1024]{1,0:T(8,128)(2,1)} %param.10) | copy-start | bytes 1572868
  68.9 134.8 %all-to-all-start = ((bf16[32,1,64,1024]{3,2,1,0:T(8,128)(2,1)}), bf16[32,1,64,1024]{3,2,1,0:T(8,128)(2,1)}, u32[]{:S(2)}, u32[]{:S(2)}) async-start(bf16[32,1,64,1024]{3,2,1,0:T(8,128)(2,1)} %bitcast_select_fusion.4), calls=%async_computation | async-start | bytes 8388608 | tf_op jit(solution)/shard_map/all_to_all | solution.py:55
  78.0 5.6 %copy-start.4 = (s32[2,8,16]{2,1,0:T(8,128)S(1)}, s32[2,8,16]{2,1,0:T(8,128)}, u32[]{:S(2)}) copy-start(s32[2,8,16]{2,1,0:T(8,128)} %param.15) | copy-start | bytes 3076
  279.4 1.0 copy-start.1
Sparse Core Ops, SparseCore 0:
  20.3 181.5 all-gather.2
where the time goes:
time: 288 us; the launch traced here: 287 us
  waiting for transfers between devices  118 us (41%)
  matrix products  55.1 us (19%)
  blocking collectives  53.9 us (19%)
  local copies, waits for them, and re-layouts  29.1 us (10%)
  between operations  13.5 us (5%)
  other arithmetic  9.49 us (3%)
  starting transfers between devices  8.12 us (3%)
    all_to_all x1, waiting for transfers between devices, local(): lax.all_to_all(outgoing, 'member', split_axis=0, concat_axis=0, tiled=True)  118 us
    all_gather x1, blocking collectives, local(): lax.all_gather(wanted.reshape(1, requests), 'member', axis=0, tiled=True)  40.2 us
    sub x2, matrix products, attend(): expd = jnp.exp(scores - peak)  25.1 us
    dot_general x2, matrix products, attend(): jnp.einsum('kgts,skd->tkgd', probs, value_block, preferred_element_type=j...  20.9 us
    all_gather x1, blocking collectives, local(): head_columns = lax.all_gather(w_kv, 'group', axis=1, tiled=True)  13.6 us
    dynamic_update_slice x4, local copies, waits for them, and re-layouts, local(): results = lax.map(attend, (queries, keys, values))  8.71 us
    all_to_all x1, starting transfers between devices, local(): lax.all_to_all(outgoing, 'member', split_axis=0, concat_axis=0, tiled=True)  8.12 us
    unnamed x14, local copies, waits for them, and re-layouts  7.19 us
  transfers between devices with their start and end apart: 2, of which 1 were waited for; matrix products, arithmetic and copies ran while one was open for 7% of the time, Pallas kernels for 0%

commit v1 on v0

--- a/solution.py
+++ b/solution.py
@@ -26,7 +26,16 @@
     normed = (
         hidden * lax.rsqrt(jnp.mean(hidden * hidden, axis=1, keepdims=True) + EPSILON)
     ).astype(jnp.bfloat16)
-    head_columns = lax.all_gather(w_kv, "group", axis=1, tiled=True)
+    ways = lax.axis_size("group")
+    up = [(d, (d + 1) % ways) for d in range(ways)]
+    down = [(d, (d - 1) % ways) for d in range(ways)]
+    earlier, later = ([w_kv], [w_kv])
+    for _ in range(ways // 2):
+        earlier.append(lax.ppermute(earlier[-1], "group", up))
+    for _ in range((ways - 1) // 2):
+        later.append(lax.ppermute(later[-1], "group", down))
+    line = jnp.concatenate([*earlier[::-1], *later[1:]], axis=1)
+    head_columns = jnp.roll(line, (lax.axis_index("group") - ways // 2) * w_kv.shape[1], axis=1)
     projected = jnp.dot(
         normed,
         lax.all_gather(head_columns, "member", axis=0, tiled=True),

time: 288 us -> 295 us (1.024); the launches traced: 287 us -> 291 us
  blocking collectives: 53.9 us -> 40.2 us
  starting transfers between devices: 8.12 us -> 16.9 us
  waiting for transfers between devices: 118 us -> 124 us
    all_gather x1 -> x0, blocking collectives: 13.6 us -> none  [local(): head_columns = lax.all_gather(w_kv, 'group', axis=1, tiled=True)]
    ppermute x0 -> x7, waiting for transfers between devices: none -> 9.65 us  [the longest x4 9.12 us: local(): earlier.append(lax.ppermute(earlier[-1], 'group', up))]
    ppermute x0 -> x7, starting transfers between devices: none -> 8.76 us  [the longest x3 8.75 us: local(): later.append(lax.ppermute(later[-1], 'group', down))]
    all_to_all x1, waiting for transfers between devices: 118 us -> 114 us  [local(): lax.all_to_all(outgoing, 'member', split_axis=0, concat_axis=0, tiled=True)]
    unnamed x14 -> x29, local copies, waits for them, and re-layouts: 7.19 us -> 8.94 us
  transfers between devices with their start and end apart: 2 -> 9, of which waited for: 1 -> 7; matrix products, arithmetic and copies ran while one was open for 7% -> 7% of each run, Pallas kernels for 0% -> 0%
where the time goes in v1:
time: 295 us; the launch traced here: 291 us
  waiting for transfers between devices  124 us (42%)
  matrix products  55 us (19%)
  blocking collectives  40.2 us (14%)
  local copies, waits for them, and re-layouts  31.6 us (11%)
  starting transfers between devices  16.9 us (6%)
  between operations  13.6 us (5%)
  other arithmetic  9.48 us (3%)
    all_to_all x1, waiting for transfers between devices, local(): lax.all_to_all(outgoing, 'member', split_axis=0, concat_axis=0, tiled=True)  114 us
    all_gather x1, blocking collectives, local(): lax.all_gather(wanted.reshape(1, requests), 'member', axis=0, tiled=True)  40.2 us
    sub x2, matrix products, attend(): expd = jnp.exp(scores - peak)  25.1 us
    dot_general x2, matrix products, attend(): jnp.einsum('kgts,skd->tkgd', probs, value_block, preferred_element_type=j...  20.8 us
    ppermute x4, waiting for transfers between devices, local(): earlier.append(lax.ppermute(earlier[-1], 'group', up))  9.12 us
    unnamed x29, local copies, waits for them, and re-layouts  8.94 us
    ppermute x3, starting transfers between devices, local(): later.append(lax.ppermute(later[-1], 'group', down))  8.75 us
    dynamic_update_slice x4, local copies, waits for them, and re-layouts, local(): results = lax.map(attend, (queries, keys, values))  8.71 us
  transfers between devices with their start and end apart: 9, of which 7 were waited for; matrix products, arithmetic and copies ran while one was open for 7% of the time, Pallas kernels for 0%

profile of v1, /device:TPU:32, one launch (start us, length us, event | category | flops | bytes accessed | tf_op | source)
XLA Modules:
  0.0 290.6 jit_solution(5135085794439269366)
XLA Ops:
  6.5 4.8 %collective-permute-done = bf16[128,128]{1,0:T(8,128)(2,1)S(1)} collective-permute-done((bf16[128,128]{1,0:T(8,128)(2,1)}, bf16[128,128]{1,0:T(8,128)(2,1)S(1)}, u32[]{:S(2)}, u32[]{:S(2)}) %collective-permute-start) | collective-permute-done | bytes 32800 | tf_op jit(solution)/shard_map/ppermute | solution.py:34
  11.3 3.0 %collective-permute-start.4 = (bf16[128,128]{1,0:T(8,128)(2,1)}, bf16[128,128]{1,0:T(8,128)(2,1)S(1)}, u32[]{:S(2)}, u32[]{:S(2)}) collective-permute-start(bf16[128,128]{1,0:T(8,128)(2,1)} %param.13), channel_id=1, source_target_pairs={{0,224},{32,0},{64,32},{96,64},{128,96},{160,128},{192,160},{224,1... | collective-permute-start | bytes 98312 | tf_op jit(solution)/shard_map/ppermute | solution.py:36
  16.2 2.8 collective-permute-start.5
  20.6 3.0 %collective-permute-start.6 = (bf16[128,128]{1,0:T(8,128)(2,1)S(1)}, bf16[128,128]{1,0:T(8,128)(2,1)S(1)}, u32[]{:S(2)}, u32[]{:S(2)}) collective-permute-start(bf16[128,128]{1,0:T(8,128)(2,1)S(1)} %collective-permute-done.5), channel_id=1, source_target_pairs={{0,224},{32,0},{64,32},{96,64},{128,96},{160,128},{192,160},{224,1... | collective-permute-start | bytes 98312 | tf_op jit(solution)/shard_map/ppermute | solution.py:36
  28.3 40.2 %all-gather = s32[32,1,16]{2,1,0:T(1,128)S(1)} all-gather(s32[1,1,16]{2,1,0:T(1,128)S(1)} %reshape.252), channel_id=1, replica_groups=mesh['group'=8,'member'=32] {'member'}, dimensions={0}, use_global_device_ids=true | all-gather | bytes 2112 | tf_op jit(solution)/shard_map/all_gather | solution.py:50
  68.8 2.8 gather_fusion
  71.7 4.5 %bitcast_select_fusion.4 = bf16[32,1,64,1024]{3,2,1,0:T(8,128)(2,1)} fusion(bf16[32,64,1024]{2,1,0:T(8,128)(2,1)} %gather_fusion, pred[32]{0:T(512)(128)(4,1)S(1)} %reduce_or.19), kind=kLoop, calls=%fused_computation.31 | loop fusion | flops 2097152 | bytes 8388640 | tf_op jit(solution)/shard_map/jit(_where)/select_n | solution.py:61
  76.2 8.1 %all-to-all-start = ((bf16[32,1,64,1024]{3,2,1,0:T(8,128)(2,1)}), bf16[32,1,64,1024]{3,2,1,0:T(8,128)(2,1)}, u32[]{:S(2)}, u32[]{:S(2)}) async-start(bf16[32,1,64,1024]{3,2,1,0:T(8,128)(2,1)} %bitcast_select_fusion.4), calls=%async_computation | async-start | bytes 8388608 | tf_op jit(solution)/shard_map/all_to_all | solution.py:64
  85.3 5.4 %copy.46 = bf16[32,8,64,128]{3,2,1,0:T(8,128)(2,1)} copy(bf16[32,8,64,128]{3,1,2,0:T(8,128)(2,1)} %bitcast.134) | data formatting | bytes 8388608
  91.1 1.9 fusion.30
  93.0 114.1 %all-to-all-done = bf16[32,1,64,1024]{3,2,1,0:T(8,128)(2,1)} async-done(((bf16[32,1,64,1024]{3,2,1,0:T(8,128)(2,1)}), bf16[32,1,64,1024]{3,2,1,0:T(8,128)(2,1)}, u32[]{:S(2)}, u32[]{:S(2)}) %all-to-all-start) | async-done | bytes 4194336 | tf_op jit(solution)/shard_map/all_to_all | solution.py:64
  207.2 2.9 gather_fusion.1
  210.1 6.3 %convolution_convert_fusion = bf16[256,1024]{1,0:T(8,128)(2,1)S(1)} fusion(bf16[256,4096]{1,0:T(8,128)(2,1)} %fusion.30, bf16[4096,1024]{1,0:T(8,128)(2,1)} %all-gather.3.cloned.1.call-done), kind=kOutput, calls=%fused_computation.40 | convolution fusion | flops 2147745792 | bytes 11010048 | tf_op jit(solution)/shard_map/dot_general | solution.py:39
  216.4 2.6 convert_select_fusion
  219.0 2.9 copy.34
  223.6 59.1 %while.11 = (s32[]{:T(128)}, bf16[2,128,8192]{2,1,0:T(8,128)(2,1)}, bf16[2,640,4,128]{1,3,2,0:T(8,128)(2,1)}, bf16[2,640,4,128]{1,3,2,0:T(8,128)(2,1)}, bf16[2,1...) while((s32[]{:T(128)}, bf16[2,128,8192]{2,1,0:T(8,128)(2,1)}, ...), condition=%wide.region_8.9_spmd.clone, body=%wide.region_5.8_spmd.clone.sunk | while | flops 2717024768 | bytes 60265176 | solution.py:104
  223.6 2.0 constant_dynamic-slice_fusion.3
  225.8 12.5 %fusion.73 = (f32[4,16,128]{2,1,0:T(8,128)S(1)}, f32[4,16,128,640]{2,3,1,0:T(8,128)}) fusion(pred[128,640]{0,1:T(8,128)(4,1)S(1)} %fusion.72, bf16[1,128,4,16,128]{4,3,2,1,0:T(8,128)(2,1)S(1)} %constant_dynamic-slice_fusion.3, bf16[2,640,4,128]{1,3,2,0:T(8,128)(2,1)} %get-tuple-element.170, s32[]{:T(128)} %get-tuple-element.159), kind=kOutput, calls=%fused_computation.109.clone.1 | convolution fusion | flops 1363149440 | bytes 23839232 | tf_op jit(solution)/shard_map/while/body/eval_jaxpr/sub | solution.py:97
  238.4 10.4 %fusion.74 = bf16[4,128,16,128]{3,1,2,0:T(8,128)(2,1)} fusion(f32[4,16,128,640]{2,3,1,0:T(8,128)} %get-tuple-element.149, f32[4,16,128]{2,1,0:T(8,128)S(1)} %get-tuple-element.150, bf16[2,640,4,128]{1,3,2,0:T(8,128)(2,1)} %get-tuple-element.169, s32[]{:T(128)} %get-tuple-element.159), kind=kOutput, calls=%fused_computation.14.clone.1 | convolution fusion | flops 1353711616 | bytes 23757312 | tf_op jit(solution)/shard_map/while/body/eval_jaxpr/kgts,skd->tkgd/dot_general | solution.py:99
  248.8 2.9 copy.61
  253.2 2.0 constant_dynamic-slice_fusion.3
  255.4 12.5 %fusion.73 = (f32[4,16,128]{2,1,0:T(8,128)S(1)}, f32[4,16,128,640]{2,3,1,0:T(8,128)}) fusion(pred[128,640]{0,1:T(8,128)(4,1)S(1)} %fusion.72, bf16[1,128,4,16,128]{4,3,2,1,0:T(8,128)(2,1)S(1)} %constant_dynamic-slice_fusion.3, bf16[2,640,4,128]{1,3,2,0:T(8,128)(2,1)} %get-tuple-element.170, s32[]{:T(128)} %get-tuple-element.159), kind=kOutput, calls=%fused_computation.109.clone.1 | convolution fusion | flops 1363149440 | bytes 23839232 | tf_op jit(solution)/shard_map/while/body/eval_jaxpr/sub | solution.py:97
  267.9 10.4 %fusion.74 = bf16[4,128,16,128]{3,1,2,0:T(8,128)(2,1)} fusion(f32[4,16,128,640]{2,3,1,0:T(8,128)} %get-tuple-element.149, f32[4,16,128]{2,1,0:T(8,128)S(1)} %get-tuple-element.150, bf16[2,640,4,128]{1,3,2,0:T(8,128)(2,1)} %get-tuple-element.169, s32[]{:T(128)} %get-tuple-element.159), kind=kOutput, calls=%fused_computation.14.clone.1 | convolution fusion | flops 1353711616 | bytes 23757312 | tf_op jit(solution)/shard_map/while/body/eval_jaxpr/kgts,skd->tkgd/dot_general | solution.py:99
  278.4 2.9 copy.61
  (67 shorter events, 16.0 us)
Async XLA Ops:
  6.5 62.3 %copy-start = (bf16[4,64,1024]{2,1,0:T(8,128)(2,1)S(1)}, bf16[4,64,1024]{2,1,0:T(8,128)(2,1)}, u32[]{:S(2)}) copy-start(bf16[4,64,1024]{2,1,0:T(8,128)(2,1)} %param.11) | copy-start | bytes 1572868
  6.5 203.5 %all-gather.3.cloned.1.call-start = ((), (), s32[]{:S(2)}) async-start(), calls=%async_computation.1 | async-start | bytes 8650752 | tf_op jit(solution)/shard_map/all_gather | solution.py:41
  6.5 4.8 %collective-permute-start = (bf16[128,128]{1,0:T(8,128)(2,1)}, bf16[128,128]{1,0:T(8,128)(2,1)S(1)}, u32[]{:S(2)}, u32[]{:S(2)}) collective-permute-start(bf16[128,128]{1,0:T(8,128)(2,1)} %param.13), channel_id=1, source_target_pairs={{0,32},{32,64},{64,96},{96,128},{128,160},{160,192},{192,224},{224... | collective-permute-start | bytes 98312 | tf_op jit(solution)/shard_map/ppermute | solution.py:34
  11.3 4.6 %collective-permute-start.1 = (bf16[128,128]{1,0:T(8,128)(2,1)S(1)}, bf16[128,128]{1,0:T(8,128)(2,1)S(1)}, u32[]{:S(2)}, u32[]{:S(2)}) collective-permute-start(bf16[128,128]{1,0:T(8,128)(2,1)S(1)} %collective-permute-done), channel_id=1, source_target_pairs={{0,32},{32,64},{64,96},{96,128},{128,160},{160,192},{192,224},{224... | collective-permute-start | bytes 98312 | tf_op jit(solution)/shard_map/ppermute | solution.py:34
  11.3 4.9 %collective-permute-start.4 = (bf16[128,128]{1,0:T(8,128)(2,1)}, bf16[128,128]{1,0:T(8,128)(2,1)S(1)}, u32[]{:S(2)}, u32[]{:S(2)}) collective-permute-start(bf16[128,128]{1,0:T(8,128)(2,1)} %param.13), channel_id=1, source_target_pairs={{0,224},{32,0},{64,32},{96,64},{128,96},{160,128},{192,160},{224,1... | collective-permute-start | bytes 98312 | tf_op jit(solution)/shard_map/ppermute | solution.py:36
  15.9 4.6 %collective-permute-start.2 = (bf16[128,128]{1,0:T(8,128)(2,1)S(1)}, bf16[128,128]{1,0:T(8,128)(2,1)S(1)}, u32[]{:S(2)}, u32[]{:S(2)}) collective-permute-start(bf16[128,128]{1,0:T(8,128)(2,1)S(1)} %collective-permute-done.1), channel_id=1, source_target_pairs={{0,32},{32,64},{64,96},{96,128},{128,160},{160,192},{192,224},{224... | collective-permute-start | bytes 98312 | tf_op jit(solution)/shard_map/ppermute | solution.py:34
  16.2 4.4 %collective-permute-start.5 = (bf16[128,128]{1,0:T(8,128)(2,1)S(1)}, bf16[128,128]{1,0:T(8,128)(2,1)S(1)}, u32[]{:S(2)}, u32[]{:S(2)}) collective-permute-start(bf16[128,128]{1,0:T(8,128)(2,1)S(1)} %collective-permute-done.4), channel_id=1, source_target_pairs={{0,224},{32,0},{64,32},{96,64},{128,96},{160,128},{192,160},{224,1... | collective-permute-start | bytes 98312 | tf_op jit(solution)/shard_map/ppermute | solution.py:36
  20.4 4.6 %collective-permute-start.3 = (bf16[128,128]{1,0:T(8,128)(2,1)S(1)}, bf16[128,128]{1,0:T(8,128)(2,1)S(1)}, u32[]{:S(2)}, u32[]{:S(2)}) collective-permute-start(bf16[128,128]{1,0:T(8,128)(2,1)S(1)} %collective-permute-done.2), channel_id=1, source_target_pairs={{0,32},{32,64},{64,96},{96,128},{128,160},{160,192},{192,224},{224... | collective-permute-start | bytes 98312 | tf_op jit(solution)/shard_map/ppermute | solution.py:34
  20.6 5.2 %collective-permute-start.6 = (bf16[128,128]{1,0:T(8,128)(2,1)S(1)}, bf16[128,128]{1,0:T(8,128)(2,1)S(1)}, u32[]{:S(2)}, u32[]{:S(2)}) collective-permute-start(bf16[128,128]{1,0:T(8,128)(2,1)S(1)} %collective-permute-done.5), channel_id=1, source_target_pairs={{0,224},{32,0},{64,32},{96,64},{128,96},{160,128},{192,160},{224,1... | collective-permute-start | bytes 98312 | tf_op jit(solution)/shard_map/ppermute | solution.py:36
  76.2 8.1 %copy-start.5 = (s32[2,8]{1,0:T(2,128)S(1)}, s32[2,8]{1,0:T(2,128)}, u32[]{:S(2)}) copy-start(s32[2,8]{1,0:T(2,128)} %param.14) | copy-start | bytes 196
  76.2 8.3 %copy-start.2 = (bf16[2,8,16,4096]{3,2,1,0:T(8,128)(2,1)S(1)}, bf16[2,8,16,4096]{3,2,1,0:T(8,128)(2,1)}, u32[]{:S(2)}) copy-start(bf16[2,8,16,4096]{3,2,1,0:T(8,128)(2,1)} %param.12) | copy-start | bytes 6291460
  76.2 8.9 %copy-start.3 = (bf16[256,1024]{1,0:T(8,128)(2,1)S(1)}, bf16[256,1024]{1,0:T(8,128)(2,1)}, u32[]{:S(2)}) copy-start(bf16[256,1024]{1,0:T(8,128)(2,1)} %param.10) | copy-start | bytes 1572868
  76.2 131.0 %all-to-all-start = ((bf16[32,1,64,1024]{3,2,1,0:T(8,128)(2,1)}), bf16[32,1,64,1024]{3,2,1,0:T(8,128)(2,1)}, u32[]{:S(2)}, u32[]{:S(2)}) async-start(bf16[32,1,64,1024]{3,2,1,0:T(8,128)(2,1)} %bitcast_select_fusion.4), calls=%async_computation | async-start | bytes 8388608 | tf_op jit(solution)/shard_map/all_to_all | solution.py:64
  85.3 5.6 %copy-start.4 = (s32[2,8,16]{2,1,0:T(8,128)S(1)}, s32[2,8,16]{2,1,0:T(8,128)}, u32[]{:S(2)}) copy-start(s32[2,8,16]{2,1,0:T(8,128)} %param.15) | copy-start | bytes 3076
  282.7 1.0 copy-start.1
Sparse Core Ops, SparseCore 0:
  27.6 177.2 all-gather.2
